TPU v7x, 256 devices: a whole 4x4x8 slice. The times are simulated.
256 devices in a mesh: seq: 32 (over y, z), grp: 8 (over x, core).
Axes of the slice: x: 4, y: 4, z: 8, core: 2. Of those that a mesh axis runs over, the one named last changes fastest.
Arguments:
- mixer_input: bfloat16 [5120, 32768], P('grp', 'seq'), may hold values from -5 to 5
- step_sizes: float32 [80, 32768], P('grp', 'seq'), may hold values from 0 to 1, as said below
- decay_rates: float32 [80], P('grp'), may hold values from 1 to 2
- skip_gain: float32 [80], P('grp'), may hold values from 0.5 to 1.5
- input_basis: bfloat16 [32768, 128], P('seq'), may hold values from -5 to 5
- output_basis: bfloat16 [32768, 128], P('seq'), may hold values from -0.5 to 0.5
- out_weight: bfloat16 [5120, 2560], P(None, 'grp'), may hold values from -0.078125 to 0.078125
Outputs:
- layer_output: bfloat16 [32768, 2560], P('seq', 'grp')
Inputs may be any that keep to these rules, and one draw needn't show every extreme that they name: `step_sizes`: positive step sizes.
All inputs are finite; a program needn't handle non-finite values.
Results may differ from a plain program's by a relative error of at most 0.0065.
Values may be sent and summed in bfloat16 or wider, within the bound.
A program may use at most 128 MiB of HBM per device.

v0:
```python
import jax
import jax.numpy as jnp
from jax import lax
from jax.sharding import PartitionSpec as P

HP = 64
N = 128
GROUP = 256


def carry_in(total_log, final_state):
    peers, here = (lax.axis_size("seq"), lax.axis_index("seq"))

    def shifted(value, d):
        return lax.ppermute(value, "seq", [(i, i + d) for i in range(peers - d)])

    decay = shifted(jnp.exp(total_log), 1)
    decay = jnp.where(here >= 1, decay, jnp.ones_like(decay))
    state = shifted(final_state, 1)
    d = 1
    while d < peers:
        decay_r, state_r = (shifted(decay, d), shifted(state, d))
        reached = here >= d
        state = jnp.where(reached, decay[:, None, None] * state_r + state, state)
        decay = jnp.where(reached, decay * decay_r, decay)
        d *= 2
    return state


def on_device(
    mixer_input, step_sizes, decay_rates, skip_gain, input_basis, output_basis, out_weight
):
    heads_here = step_sizes.shape[0]
    tokens_here = step_sizes.shape[1]
    count = tokens_here // GROUP
    channels = mixer_input.reshape(heads_here, HP, count, GROUP)
    log_decay = -(decay_rates[:, None] * step_sizes).reshape(heads_here, count, GROUP)
    steps_blocked = step_sizes.reshape(heads_here, count, GROUP)
    running = jnp.cumsum(log_decay, axis=2)
    basis_in_blocked = input_basis.reshape(count, GROUP, N)
    basis_out_blocked = output_basis.reshape(count, GROUP, N)
    gram = jnp.einsum(
        "cin,cjn->cij", basis_out_blocked, basis_in_blocked, preferred_element_type=jnp.float32
    )
    rows_index = lax.broadcasted_iota(jnp.int32, (GROUP, GROUP), 0)
    cols_index = lax.broadcasted_iota(jnp.int32, (GROUP, GROUP), 1)
    causal = rows_index >= cols_index
    gaps = running[:, :, :, None] - running[:, :, None, :]
    mixing = jnp.where(
        causal,
        gram[None] * jnp.exp(jnp.where(causal, gaps, 0.0)) * steps_blocked[:, :, None, :],
        0.0,
    ).astype(jnp.bfloat16)
    inner = jnp.einsum("hcij,hpcj->hpci", mixing, channels, preferred_element_type=jnp.float32)
    tail = jnp.exp(running[:, :, -1:] - running) * steps_blocked
    weighted_terms = (basis_in_blocked.astype(jnp.float32)[None] * tail[:, :, :, None]).astype(
        jnp.bfloat16
    )
    summaries = jnp.einsum(
        "hcjn,hpcj->chnp", weighted_terms, channels, preferred_element_type=jnp.float32
    )
    block_decay = jnp.exp(running[:, :, -1])

    def advance(state, pair):
        decay, digest_record = pair
        return (decay[:, None, None] * state + digest_record, state)

    zero_state = jnp.zeros((heads_here, N, HP), jnp.float32)
    final_state, entering = lax.scan(advance, zero_state, (block_decay.T, summaries))
    block_sums = jnp.sum(log_decay, axis=2)
    prefix = jnp.exp(jnp.cumsum(block_sums, axis=1) - block_sums)
    total_log = jnp.sum(block_sums, axis=1)
    basis_out_wide = basis_out_blocked.astype(jnp.float32)
    within = jnp.exp(running)[:, None]
    direct = skip_gain[:, None, None, None] * channels.astype(jnp.float32)
    carried = carry_in(total_log, final_state)
    states = entering + prefix.T[:, :, None, None] * carried[None]
    from_state = jnp.einsum(
        "cin,chnp->hpci", basis_out_wide, states, precision=lax.Precision.HIGHEST
    )
    mixed = inner + from_state * within + direct
    mixed_columns = mixed.astype(jnp.bfloat16).reshape(heads_here * HP, tokens_here)
    result = jnp.einsum(
        "kt,kd->td",
        lax.all_gather(mixed_columns, "grp", axis=0, tiled=True),
        out_weight,
        preferred_element_type=jnp.float32,
    )
    return result.astype(jnp.bfloat16)


def solution(mesh):
    placed = (
        P("grp", "seq"),
        P("grp", "seq"),
        P("grp"),
        P("grp"),
        P("seq", None),
        P("seq", None),
        P(None, "grp"),
    )
    return jax.shard_map(
        on_device, mesh=mesh, in_specs=placed, out_specs=P("seq", "grp"), check_vma=False
    )
```

profile of v0, /device:TPU:1, one launch (start us, length us, event | category | flops | bytes accessed | tf_op | source)
XLA Modules:
  0.0 231.2 jit_solution(14767401530149646596)
XLA Ops:
  6.5 1.0 mul.141
  7.6 1.0 fusion.19
  8.6 0.6 copy-done.5
  9.3 2.3 reduce-window.6
  11.6 0.2 slice_reduce_fusion
  11.8 0.1 broadcast_add_fusion
  12.0 0.1 slice.15
  12.1 0.1 copy.33
  12.2 0.1 copy.34
  12.3 0.6 fusion.20
  12.9 1.8 convert_element_type.24
  14.7 3.8 %reshape.94 = bf16[10,64,4,256]{3,2,1,0:T(4,128)(2,1)} reshape(bf16[640,1024]{1,0:T(8,128)(2,1)} %param.9) | data formatting | bytes 2621440 | tf_op jit(solution)/shard_map/reshape | solution.py:36
  18.5 5.6 %fusion.8 = f32[4,10,128,64]{3,2,1,0:T(8,128)} fusion(f32[10,4,256]{2,0,1:T(8,128)S(1)} %copy.35, f32[4,256,128]{2,1,0:T(8,128)} %convert_element_type.24, bf16[10,64,4,256]{3,2,1,0:T(4,128)(2,1)} %reshape.94), kind=kOutput, calls=%fused_computation.13 | convolution fusion | flops 170393600 | bytes 3186688 | tf_op jit(solution)/shard_map/hcjn,hpcj->chnp/dot_general | solution.py:59
  24.1 15.7 %while.13 = (s32[]{:T(128)}, f32[10,128,64]{2,1,0:T(8,128)}, f32[4,10,128,64]{3,2,1,0:T(8,128)}, f32[4,10]{1,0:T(4,128)S(1)}, f32[4,10,128,64]{3,2,1,0:T(8,128)}, /*index=5*/s32[]{:T(128)}, s32[]{:T(128)}) while((s32[]{:T(128)}, f32[10,128,64]{2,1,0:T(8,128)}, f32[4,10,128,64]{3,2,1,0:T(8,128)}, f32[4,10]{1,0:T(4,128)S(1)}, ...), condition=%wide.region_3.4_spmd.clone, body=%wide.region_2.3_spmd.clone.sunk | while | flops 327683 | bytes 2293988 | solution.py:69
  24.1 0.9 bitcast_dynamic-update-slice_fusion.2
  25.1 2.1 bitcast_add_fusion.2
  27.1 2.0 bitcast_dynamic-update-slice_fusion.2
  29.1 2.3 bitcast_add_fusion.2
  31.4 2.0 bitcast_dynamic-update-slice_fusion.2
  33.4 2.3 bitcast_add_fusion.2
  35.6 2.0 bitcast_dynamic-update-slice_fusion.2
  37.6 2.3 bitcast_add_fusion.2
  39.9 2.1 copy.39
  41.9 5.1 %collective-permute-start.5 = (f32[10,128,64]{1,2,0:T(8,128)}, f32[10,128,64]{1,2,0:T(8,128)}, u32[]{:S(2)}, u32[]{:S(2)}) collective-permute-start(f32[10,128,64]{1,2,0:T(8,128)} %copy.39), channel_id=1, source_target_pairs={{0,8},{8,16},{16,24},{24,32},{32,40},{40,48},{48,56},{56,64},{64,7... | collective-permute-start | bytes 983048 | tf_op jit(solution)/shard_map/ppermute | solution.py:15
  47.0 6.0 %collective-permute-done.5 = f32[10,128,64]{1,2,0:T(8,128)} collective-permute-done((f32[10,128,64]{1,2,0:T(8,128)}, f32[10,128,64]{1,2,0:T(8,128)}, u32[]{:S(2)}, u32[]{:S(2)}) %collective-permute-start.5) | collective-permute-done | bytes 327712 | tf_op jit(solution)/shard_map/ppermute | solution.py:15
  53.0 4.8 %collective-permute-start.6 = (f32[10,128,64]{1,2,0:T(8,128)}, f32[10,128,64]{1,2,0:T(8,128)}, u32[]{:S(2)}, u32[]{:S(2)}) collective-permute-start(f32[10,128,64]{1,2,0:T(8,128)} %collective-permute-done.5), channel_id=1, source_target_pairs={{0,8},{8,16},{16,24},{24,32},{32,40},{40,48},{48,56},{56,64},{64,7... | collective-permute-start | bytes 983048 | tf_op jit(solution)/shard_map/ppermute | solution.py:15
  57.8 2.8 %collective-permute-start = (f32[10]{0:T(128)S(1)}, f32[10]{0:T(128)S(1)}, u32[]{:S(2)}, u32[]{:S(2)}) collective-permute-start(f32[10]{0:T(128)S(1)} %negate_exponential_fusion), channel_id=1, source_target_pairs={{0,8},{8,16},{16,24},{24,32},{32,40},{40,48},{48,56},{56,64},{64,7... | collective-permute-start | bytes 128 | tf_op jit(solution)/shard_map/ppermute | solution.py:15
  60.7 2.2 collective-permute-done
  62.8 0.0 collective-permute-done.6
  62.9 1.9 add_select_fusion.4
  64.8 6.6 %collective-permute-start.7 = (f32[10,128,64]{1,2,0:T(8,128)}, f32[10,128,64]{1,2,0:T(8,128)}, u32[]{:S(2)}, u32[]{:S(2)}) collective-permute-start(f32[10,128,64]{1,2,0:T(8,128)} %add_select_fusion.4), channel_id=1, source_target_pairs={{0,16},{8,24},{16,32},{24,40},{32,48},{40,56},{48,64},{56,72},{64,... | collective-permute-start | bytes 983048 | tf_op jit(solution)/shard_map/ppermute | solution.py:15
  71.3 5.0 %collective-permute-start.1 = (f32[10]{0:T(128)S(1)}, f32[10]{0:T(128)S(1)}, u32[]{:S(2)}, u32[]{:S(2)}) collective-permute-start(f32[10]{0:T(128)S(1)} %broadcast_select_fusion.1), channel_id=1, source_target_pairs={{0,8},{8,16},{16,24},{24,32},{32,40},{40,48},{48,56},{56,64},{64,7... | collective-permute-start | bytes 128 | tf_op jit(solution)/shard_map/ppermute | solution.py:15
  76.3 0.7 collective-permute-done.1
  77.0 1.9 add_select_fusion.3
  79.0 20.3 %collective-permute-start.8 = (f32[10,128,64]{1,2,0:T(8,128)}, f32[10,128,64]{1,2,0:T(8,128)}, u32[]{:S(2)}, u32[]{:S(2)}) collective-permute-start(f32[10,128,64]{1,2,0:T(8,128)} %add_select_fusion.3), channel_id=1, source_target_pairs={{0,32},{8,40},{16,48},{24,56},{32,64},{40,72},{48,80},{56,88},{64,... | collective-permute-start | bytes 983048 | tf_op jit(solution)/shard_map/ppermute | solution.py:15
  99.3 2.2 fusion.22
  101.5 1.5 reshape.95
  103.0 0.9 reduce_sum.18
  103.9 0.8 reduce_window_sum.43
  104.7 1.3 collective-permute-start.2
  106.0 7.2 %collective-permute-done.2 = f32[10]{0:T(128)S(1)} collective-permute-done((f32[10]{0:T(128)}, f32[10]{0:T(128)S(1)}, u32[]{:S(2)}, u32[]{:S(2)}) %collective-permute-start.2) | collective-permute-done | bytes 72 | tf_op jit(solution)/shard_map/ppermute | solution.py:15
  113.1 0.7 broadcast_select_fusion.2
  113.8 1.9 add_select_fusion.2
  115.7 5.6 %collective-permute-start.9 = (f32[10,128,64]{1,2,0:T(8,128)}, f32[10,128,64]{1,2,0:T(8,128)}, u32[]{:S(2)}, u32[]{:S(2)}) collective-permute-start(f32[10,128,64]{1,2,0:T(8,128)} %add_select_fusion.2), channel_id=1, source_target_pairs={{0,64},{8,72},{16,80},{24,88},{32,96},{40,104},{48,112},{56,120},{... | collective-permute-start | bytes 983048 | tf_op jit(solution)/shard_map/ppermute | solution.py:15
  121.3 0.7 exponential_bitcast_fusion
  122.0 0.1 copy.38
  122.1 3.8 %collective-permute-start.3 = (f32[10]{0:T(128)}, f32[10]{0:T(128)S(1)}, u32[]{:S(2)}, u32[]{:S(2)}) collective-permute-start(f32[10]{0:T(128)} %copy-done.13), channel_id=1, source_target_pairs={{0,32},{8,40},{16,48},{24,56},{32,64},{40,72},{48,80},{56,88},{64,... | collective-permute-start | bytes 128 | tf_op jit(solution)/shard_map/ppermute | solution.py:15
  125.9 0.9 collective-permute-done.3
  126.8 0.7 broadcast_select_fusion.3
  127.5 1.2 add_select_fusion.1
  128.7 8.7 %collective-permute-start.10 = (f32[10,128,64]{1,2,0:T(8,128)S(1)}, f32[10,128,64]{1,2,0:T(8,128)S(1)}, u32[]{:S(2)}, u32[]{:S(2)}) collective-permute-start(f32[10,128,64]{1,2,0:T(8,128)S(1)} %add_select_fusion.1), channel_id=1, source_target_pairs={{0,128},{8,136},{16,144},{24,152},{32,160},{40,168},{48,176},{56,1... | collective-permute-start | bytes 983048 | tf_op jit(solution)/shard_map/ppermute | solution.py:15
  137.4 0.6 iota_compare_fusion
  138.0 1.3 collective-permute-start.4
  139.3 3.3 %collective-permute-done.4 = f32[10]{0:T(128)S(1)} collective-permute-done((f32[10]{0:T(128)S(1)}, f32[10]{0:T(128)S(1)}, u32[]{:S(2)}, u32[]{:S(2)}) %collective-permute-start.4) | collective-permute-done | bytes 72 | tf_op jit(solution)/shard_map/ppermute | solution.py:15
  142.6 0.8 add_select_fusion
  143.5 2.0 copy.40
  145.5 0.0 copy-start.14
  145.6 4.4 %fusion.12 = f32[4,10,64,256]{3,2,0,1:T(8,128)S(1)} fusion(bf16[4,256,128,1]{2,1,0,3:T(8,128)(2,1)S(1)} %bitcast.46, f32[4,10,128,64]{3,2,1,0:T(8,128)} %get-tuple-element.33, f32[10,128,64]{2,1,0:T(8,128)} %copy.40, f32[4,10]{1,0:T(4,128)S(1)} %copy.38), kind=kOutput, calls=%fused_computation.18 | convolution fusion | flops 1007288320 | bytes 4522144 | tf_op jit(solution)/shard_map/cin,chnp->hpci/dot_general | solution.py:78
  150.0 4.0 %fusion.11 = bf16[10,64,4,256]{3,1,2,0:T(8,128)(2,1)S(1)} fusion(f32[4,10,64,256]{3,2,0,1:T(8,128)S(1)} %fusion.12, f32[10,4,256]{2,1,0:T(4,128)S(1)} %copy-done.9, f32[10,4,256]{2,1,0:T(4,128)S(1)} %copy-done.7, f32[4,256,256]{2,1,0:T(8,128)S(1)} %copy-done.2, pred[256,256]{1,0:T(8,128)(4,1)S(1)} %copy-done.10, bf16[10,64,4,256]{3,2,1,0:T(4,128)(2,1)S(1)} %copy-done.1, ...), kind=kOutput, calls=%fused_computation.17 | convolution fusion | flops 355205120 | bytes 6479912 | tf_op jit(solution)/shard_map/hcij,hpcj->hpci/dot_general | solution.py:54
  154.0 1.0 copy.43
  155.0 1.4 copy.47
  156.4 0.0 all-gather.2.cloned.1.call-update
  156.4 60.8 %all-gather.2.cloned.1.call-done = bf16[5120,1024]{1,0:T(8,128)(2,1)} async-done(((bf16[640,1024]{1,0:T(8,128)(2,1)}), bf16[5120,1024]{1,0:T(8,128)(2,1)}) %all-gather.2.cloned.1.call-update) | async-done | bytes 10485776 | tf_op jit(solution)/shard_map/all_gather | solution.py:85
  217.2 7.2 %convolution_convert_fusion = bf16[1024,320]{0,1:T(8,128)(2,1)} fusion(bf16[5120,320]{0,1:T(8,128)(2,1)S(1)} %copy-done, bf16[5120,1024]{1,0:T(8,128)(2,1)} %all-gather.2.cloned.1.call-done), kind=kOutput, calls=%fused_computation.23 | convolution fusion | flops 3355770880 | bytes 14417920 | tf_op jit(solution)/shard_map/kt,kd->td/dot_general | solution.py:83
  (53 shorter events, 0.3 us)
Async XLA Ops:
  6.5 210.6 %copy-start = (bf16[5120,320]{0,1:T(8,128)(2,1)S(1)}, bf16[5120,320]{0,1:T(8,128)(2,1)}, u32[]{:S(2)}) copy-start(bf16[5120,320]{0,1:T(8,128)(2,1)} %param.15) | copy-start | bytes 9830404
  6.5 210.6 %all-gather.2.cloned.1.call-start = ((), (), s32[]{:S(2)}) async-start(), calls=%async_computation | async-start | bytes 11796480 | tf_op jit(solution)/shard_map/all_gather | solution.py:85
  7.6 16.6 %copy-start.8 = (f32[10,4,256]{2,1,0:T(4,128)}, f32[10,4,256]{2,1,0:T(4,128)S(1)}, u32[]{:S(2)}) copy-start(f32[10,4,256]{2,1,0:T(4,128)S(1)} %mul.141) | copy-start | bytes 122884
  8.6 0.6 copy-start.5
  12.0 12.1 %copy-start.6 = (f32[10,4,256]{2,1,0:T(4,128)}, f32[10,4,256]{2,1,0:T(4,128)S(1)}, u32[]{:S(2)}) copy-start(f32[10,4,256]{2,1,0:T(4,128)S(1)} %reduce_window_sum.42) | copy-start | bytes 122884
  39.9 59.4 %copy-start.3 = (bf16[1024,128]{1,0:T(8,128)(2,1)S(1)}, bf16[1024,128]{1,0:T(8,128)(2,1)}, u32[]{:S(2)}) copy-start(bf16[1024,128]{1,0:T(8,128)(2,1)} %param.13) | copy-start | bytes 786436
  41.9 11.0 %collective-permute-start.5 = (f32[10,128,64]{1,2,0:T(8,128)}, f32[10,128,64]{1,2,0:T(8,128)}, u32[]{:S(2)}, u32[]{:S(2)}) collective-permute-start(f32[10,128,64]{1,2,0:T(8,128)} %copy.39), channel_id=1, source_target_pairs={{0,8},{8,16},{16,24},{24,32},{32,40},{40,48},{48,56},{56,64},{64,7... | collective-permute-start | bytes 983048 | tf_op jit(solution)/shard_map/ppermute | solution.py:15
  53.0 9.9 %collective-permute-start.6 = (f32[10,128,64]{1,2,0:T(8,128)}, f32[10,128,64]{1,2,0:T(8,128)}, u32[]{:S(2)}, u32[]{:S(2)}) collective-permute-start(f32[10,128,64]{1,2,0:T(8,128)} %collective-permute-done.5), channel_id=1, source_target_pairs={{0,8},{8,16},{16,24},{24,32},{32,40},{40,48},{48,56},{56,64},{64,7... | collective-permute-start | bytes 983048 | tf_op jit(solution)/shard_map/ppermute | solution.py:15
  57.8 5.0 %collective-permute-start = (f32[10]{0:T(128)S(1)}, f32[10]{0:T(128)S(1)}, u32[]{:S(2)}, u32[]{:S(2)}) collective-permute-start(f32[10]{0:T(128)S(1)} %negate_exponential_fusion), channel_id=1, source_target_pairs={{0,8},{8,16},{16,24},{24,32},{32,40},{40,48},{48,56},{56,64},{64,7... | collective-permute-start | bytes 128 | tf_op jit(solution)/shard_map/ppermute | solution.py:15
  64.8 12.3 %collective-permute-start.7 = (f32[10,128,64]{1,2,0:T(8,128)}, f32[10,128,64]{1,2,0:T(8,128)}, u32[]{:S(2)}, u32[]{:S(2)}) collective-permute-start(f32[10,128,64]{1,2,0:T(8,128)} %add_select_fusion.4), channel_id=1, source_target_pairs={{0,16},{8,24},{16,32},{24,40},{32,48},{40,56},{48,64},{56,72},{64,... | collective-permute-start | bytes 983048 | tf_op jit(solution)/shard_map/ppermute | solution.py:15
  71.3 5.7 %collective-permute-start.1 = (f32[10]{0:T(128)S(1)}, f32[10]{0:T(128)S(1)}, u32[]{:S(2)}, u32[]{:S(2)}) collective-permute-start(f32[10]{0:T(128)S(1)} %broadcast_select_fusion.1), channel_id=1, source_target_pairs={{0,8},{8,16},{16,24},{24,32},{32,40},{40,48},{48,56},{56,64},{64,7... | collective-permute-start | bytes 128 | tf_op jit(solution)/shard_map/ppermute | solution.py:15
  77.0 22.3 %copy-start.12 = (f32[10]{0:T(128)}, f32[10]{0:T(128)S(1)}, u32[]{:S(2)}) copy-start(f32[10]{0:T(128)S(1)} %broadcast_select_fusion) | copy-start | bytes 124
  79.0 34.9 %collective-permute-start.8 = (f32[10,128,64]{1,2,0:T(8,128)}, f32[10,128,64]{1,2,0:T(8,128)}, u32[]{:S(2)}, u32[]{:S(2)}) collective-permute-start(f32[10,128,64]{1,2,0:T(8,128)} %add_select_fusion.3), channel_id=1, source_target_pairs={{0,32},{8,40},{16,48},{24,56},{32,64},{40,72},{48,80},{56,88},{64,... | collective-permute-start | bytes 983048 | tf_op jit(solution)/shard_map/ppermute | solution.py:15
  101.5 44.0 %copy-start.4 = (bf16[1024,128]{1,0:T(8,128)(2,1)S(1)}, bf16[1024,128]{1,0:T(8,128)(2,1)}, u32[]{:S(2)}) copy-start(bf16[1024,128]{1,0:T(8,128)(2,1)} %param.14) | copy-start | bytes 786436
  104.7 8.5 %collective-permute-start.2 = (f32[10]{0:T(128)}, f32[10]{0:T(128)S(1)}, u32[]{:S(2)}, u32[]{:S(2)}) collective-permute-start(f32[10]{0:T(128)} %copy-done.12), channel_id=1, source_target_pairs={{0,16},{8,24},{16,32},{24,40},{32,48},{40,56},{48,64},{56,72},{64,... | collective-permute-start | bytes 128 | tf_op jit(solution)/shard_map/ppermute | solution.py:15
  113.8 1.9 copy-start.13
  115.7 11.8 %collective-permute-start.9 = (f32[10,128,64]{1,2,0:T(8,128)}, f32[10,128,64]{1,2,0:T(8,128)}, u32[]{:S(2)}, u32[]{:S(2)}) collective-permute-start(f32[10,128,64]{1,2,0:T(8,128)} %add_select_fusion.2), channel_id=1, source_target_pairs={{0,64},{8,72},{16,80},{24,88},{32,96},{40,104},{48,112},{56,120},{... | collective-permute-start | bytes 983048 | tf_op jit(solution)/shard_map/ppermute | solution.py:15
  122.1 4.7 %collective-permute-start.3 = (f32[10]{0:T(128)}, f32[10]{0:T(128)S(1)}, u32[]{:S(2)}, u32[]{:S(2)}) collective-permute-start(f32[10]{0:T(128)} %copy-done.13), channel_id=1, source_target_pairs={{0,32},{8,40},{16,48},{24,56},{32,64},{40,72},{48,80},{56,88},{64,... | collective-permute-start | bytes 128 | tf_op jit(solution)/shard_map/ppermute | solution.py:15
  128.7 13.9 %collective-permute-start.10 = (f32[10,128,64]{1,2,0:T(8,128)S(1)}, f32[10,128,64]{1,2,0:T(8,128)S(1)}, u32[]{:S(2)}, u32[]{:S(2)}) collective-permute-start(f32[10,128,64]{1,2,0:T(8,128)S(1)} %add_select_fusion.1), channel_id=1, source_target_pairs={{0,128},{8,136},{16,144},{24,152},{32,160},{40,168},{48,176},{56,1... | collective-permute-start | bytes 983048 | tf_op jit(solution)/shard_map/ppermute | solution.py:15
  138.0 4.6 %collective-permute-start.4 = (f32[10]{0:T(128)S(1)}, f32[10]{0:T(128)S(1)}, u32[]{:S(2)}, u32[]{:S(2)}) collective-permute-start(f32[10]{0:T(128)S(1)} %broadcast_select_fusion.3), channel_id=1, source_target_pairs={{0,64},{8,72},{16,80},{24,88},{32,96},{40,104},{48,112},{56,120},{... | collective-permute-start | bytes 128 | tf_op jit(solution)/shard_map/ppermute | solution.py:15
  145.5 4.4 %copy-start.1 = (bf16[10,64,4,256]{3,2,1,0:T(4,128)(2,1)S(1)}, bf16[10,64,4,256]{3,2,1,0:T(4,128)(2,1)}, u32[]{:S(2)}) copy-start(bf16[10,64,4,256]{3,2,1,0:T(4,128)(2,1)} %reshape.94) | copy-start | bytes 3932164
  145.5 4.4 %copy-start.2 = (f32[4,256,256]{2,1,0:T(8,128)S(1)}, f32[4,256,256]{2,1,0:T(8,128)}, u32[]{:S(2)}) copy-start(f32[4,256,256]{2,1,0:T(8,128)} %fusion.22) | copy-start | bytes 3145732
  145.5 4.5 %copy-start.7 = (f32[10,4,256]{2,1,0:T(4,128)S(1)}, f32[10,4,256]{2,1,0:T(4,128)}, u32[]{:S(2)}) copy-start(f32[10,4,256]{2,1,0:T(4,128)} %copy-done.6) | copy-start | bytes 122884
  145.5 4.5 %copy-start.9 = (f32[10,4,256]{2,1,0:T(4,128)S(1)}, f32[10,4,256]{2,1,0:T(4,128)}, u32[]{:S(2)}) copy-start(f32[10,4,256]{2,1,0:T(4,128)} %copy-done.8) | copy-start | bytes 122884
  145.5 4.5 %copy-start.10 = (pred[256,256]{1,0:T(8,128)(4,1)S(1)}, pred[256,256]{1,0:T(8,128)(4,1)}, u32[]{:S(2)}) copy-start(pred[256,256]{1,0:T(8,128)(4,1)} %iota_compare_fusion) | copy-start | bytes 196612
  145.5 4.5 %copy-start.11 = (f32[10,4,256]{2,1,0:T(4,128)S(1)}, f32[10,4,256]{2,1,0:T(4,128)}, u32[]{:S(2)}) copy-start(f32[10,4,256]{2,1,0:T(4,128)} %get-tuple-element.80) | copy-start | bytes 122884
  145.5 4.5 %copy-start.14 = (f32[10]{0:T(128)S(1)}, f32[10]{0:T(128)}, u32[]{:S(2)}) copy-start(f32[10]{0:T(128)} %param.12) | copy-start | bytes 124
Sparse Core Ops, SparseCore 0:
  156.5 60.5 all-gather.1
where the time goes:
time: 232 us; the launch traced here: 231 us
  waiting for transfers between devices  81 us (35%)
  starting transfers between devices  65.2 us (28%)
  other arithmetic  33.6 us (14%)
  matrix products  23.4 us (10%)
  local copies, waits for them, and re-layouts  14.2 us (6%)
  between operations  13.7 us (6%)
    ppermute x11, starting transfers between devices, shifted(): return lax.ppermute(value, 'seq', [(i, i + d) for i in range(peers - d)])  65.2 us
    all_gather x1, waiting for transfers between devices, on_device(): lax.all_gather(mixed_columns, 'grp', axis=0, tiled=True)  60.8 us
    ppermute x11, waiting for transfers between devices, shifted(): return lax.ppermute(value, 'seq', [(i, i + d) for i in range(peers - d)])  20.2 us
    add x4, other arithmetic, advance(): return (decay[:, None, None] * state + digest_record, state)  8.81 us
    select_n x5, other arithmetic, carry_in(): state = jnp.where(reached, decay[:, None, None] * state_r + state, state)  7.74 us
    dot_general x1, matrix products, on_device(): jnp.einsum('kt,kd->td', lax.all_gather(mixed_columns, 'grp', axis=0, tile...  7.17 us
    dynamic_update_slice x4, other arithmetic, on_device(): lax.scan(advance, zero_state, (block_decay.T, summaries))  6.89 us
    dot_general x1, matrix products, on_device(): jnp.einsum('hcjn,hpcj->chnp', weighted_terms, channels, preferred_element...  5.63 us
  transfers between devices with their start and end apart: 12, of which 7 were waited for; matrix products, arithmetic and copies ran while one was open for 4% of the time, Pallas kernels for 0%

commit v1 on v0

--- a/solution.py
+++ b/solution.py
@@ -6,6 +6,13 @@
 HP = 64
 N = 128
 GROUP = 256
+
+
+def perform_ladders_on_mesh(a0, lane_axis):
+    main = jnp.stack([a0 for _ in range(lax.psum(1, lane_axis))], 0)
+    x_next = lax.all_to_all(main, lane_axis, 0, 0)
+    found_now = jnp.concatenate(x_next, 0)
+    return found_now
 
 
 def carry_in(total_log, final_state):
@@ -82,7 +89,7 @@
     mixed_columns = mixed.astype(jnp.bfloat16).reshape(heads_here * HP, tokens_here)
     result = jnp.einsum(
         "kt,kd->td",
-        lax.all_gather(mixed_columns, "grp", axis=0, tiled=True),
+        perform_ladders_on_mesh(mixed_columns, "grp"),
         out_weight,
         preferred_element_type=jnp.float32,
     )

time: 232 us -> 285 us (1.23)
  blocking collectives: 0 us -> 125 us
  waiting for transfers between devices: 81 us -> 20.3 us
  between operations: 13.7 us -> 0.29 us
  local copies, waits for them, and re-layouts: 14.2 us -> 18.4 us
    all_to_all x0 -> x1, blocking collectives: none -> 125 us  [perform_ladders_on_mesh(): x_next = lax.all_to_all(main, lane_axis, 0, 0)]
    all_gather x1 -> x0, waiting for transfers between devices: 60.8 us -> none  [on_device(): lax.all_gather(mixed_columns, 'grp', axis=0, tiled=True)]
    another operation x3 -> x4, local copies, waits for them, and re-layouts: 0.08 us -> 5.4 us  [the longest x1 5.33 us: perform_ladders_on_mesh(): main = jnp.stack([a0 for _ in range(lax.psum(1, lane_axis))], 0)]
  transfers between devices with their start and end apart: 12 -> 11, of which waited for: 7 -> 6; matrix products, arithmetic and copies ran while one was open for 4% -> 3% of each run, Pallas kernels for 0% -> 0%
where the time goes in v1:
time: 285 us; the launch traced here: 283 us
  blocking collectives  125 us (44%)
  starting transfers between devices  65.3 us (23%)
  other arithmetic  33.5 us (12%)
  matrix products  20.7 us (7%)
  waiting for transfers between devices  20.3 us (7%)
  local copies, waits for them, and re-layouts  18.4 us (6%)
    all_to_all x1, blocking collectives, perform_ladders_on_mesh(): x_next = lax.all_to_all(main, lane_axis, 0, 0)  125 us
    ppermute x11, starting transfers between devices, shifted(): return lax.ppermute(value, 'seq', [(i, i + d) for i in range(peers - d)])  65.3 us
    ppermute x11, waiting for transfers between devices, shifted(): return lax.ppermute(value, 'seq', [(i, i + d) for i in range(peers - d)])  20.3 us
    add x4, other arithmetic, advance(): return (decay[:, None, None] * state + digest_record, state)  8.81 us
    select_n x5, other arithmetic, carry_in(): state = jnp.where(reached, decay[:, None, None] * state_r + state, state)  7.74 us
    dynamic_update_slice x4, other arithmetic, on_device(): lax.scan(advance, zero_state, (block_decay.T, summaries))  6.86 us
  transfers between devices with their start and end apart: 11, of which 6 were waited for; matrix products, arithmetic and copies ran while one was open for 3% of the time, Pallas kernels for 0%

profile of v1, /device:TPU:1, one launch (start us, length us, event | category | flops | bytes accessed | tf_op | source)
XLA Modules:
  0.0 283.3 jit_solution(9524548111312250898)
XLA Ops:
  0.0 1.0 mul.141
  1.0 1.0 fusion.19
  2.1 0.6 copy-done.5
  2.8 2.3 reduce-window.6
  5.1 0.2 slice_reduce_fusion
  5.3 0.1 broadcast_add_fusion
  5.5 0.1 slice.15
  5.5 0.1 copy.33
  5.6 0.1 copy.34
  5.7 0.6 fusion.20
  6.4 1.8 convert_element_type.24
  8.2 3.8 %reshape.96 = bf16[10,64,4,256]{3,2,1,0:T(4,128)(2,1)} reshape(bf16[640,1024]{1,0:T(8,128)(2,1)} %param.9) | data formatting | bytes 2621440 | tf_op jit(solution)/shard_map/reshape | solution.py:43
  12.0 5.6 %fusion.8 = f32[4,10,128,64]{3,2,1,0:T(8,128)} fusion(f32[10,4,256]{2,0,1:T(8,128)S(1)} %copy.35, f32[4,256,128]{2,1,0:T(8,128)} %convert_element_type.24, bf16[10,64,4,256]{3,2,1,0:T(4,128)(2,1)} %reshape.96), kind=kOutput, calls=%fused_computation.13 | convolution fusion | flops 170393600 | bytes 3186688 | tf_op jit(solution)/shard_map/hcjn,hpcj->chnp/dot_general | solution.py:66
  17.6 15.7 %while.13 = (s32[]{:T(128)}, f32[10,128,64]{2,1,0:T(8,128)}, f32[4,10,128,64]{3,2,1,0:T(8,128)}, f32[4,10]{1,0:T(4,128)S(1)}, f32[4,10,128,64]{3,2,1,0:T(8,128)}, /*index=5*/s32[]{:T(128)}, s32[]{:T(128)}) while((s32[]{:T(128)}, f32[10,128,64]{2,1,0:T(8,128)}, f32[4,10,128,64]{3,2,1,0:T(8,128)}, f32[4,10]{1,0:T(4,128)S(1)}, ...), condition=%wide.region_3.4_spmd.clone, body=%wide.region_2.3_spmd.clone.sunk | while | flops 327683 | bytes 2293988 | solution.py:76
  17.6 0.9 bitcast_dynamic-update-slice_fusion.2
  18.5 2.1 bitcast_add_fusion.2
  20.6 2.0 bitcast_dynamic-update-slice_fusion.2
  22.5 2.3 bitcast_add_fusion.2
  24.8 2.0 bitcast_dynamic-update-slice_fusion.2
  26.8 2.3 bitcast_add_fusion.2
  29.0 2.0 bitcast_dynamic-update-slice_fusion.2
  31.0 2.3 bitcast_add_fusion.2
  33.3 2.1 copy.39
  35.4 5.1 %collective-permute-start.5 = (f32[10,128,64]{1,2,0:T(8,128)}, f32[10,128,64]{1,2,0:T(8,128)}, u32[]{:S(2)}, u32[]{:S(2)}) collective-permute-start(f32[10,128,64]{1,2,0:T(8,128)} %copy.39), channel_id=1, source_target_pairs={{0,8},{8,16},{16,24},{24,32},{32,40},{40,48},{48,56},{56,64},{64,7... | collective-permute-start | bytes 983048 | tf_op jit(solution)/shard_map/ppermute | solution.py:22
  40.5 6.0 %collective-permute-done.5 = f32[10,128,64]{1,2,0:T(8,128)} collective-permute-done((f32[10,128,64]{1,2,0:T(8,128)}, f32[10,128,64]{1,2,0:T(8,128)}, u32[]{:S(2)}, u32[]{:S(2)}) %collective-permute-start.5) | collective-permute-done | bytes 327712 | tf_op jit(solution)/shard_map/ppermute | solution.py:22
  46.4 4.8 %collective-permute-start.6 = (f32[10,128,64]{1,2,0:T(8,128)}, f32[10,128,64]{1,2,0:T(8,128)}, u32[]{:S(2)}, u32[]{:S(2)}) collective-permute-start(f32[10,128,64]{1,2,0:T(8,128)} %collective-permute-done.5), channel_id=1, source_target_pairs={{0,8},{8,16},{16,24},{24,32},{32,40},{40,48},{48,56},{56,64},{64,7... | collective-permute-start | bytes 983048 | tf_op jit(solution)/shard_map/ppermute | solution.py:22
  51.2 2.8 collective-permute-start
  54.1 2.2 collective-permute-done
  56.3 0.0 collective-permute-done.6
  56.3 1.9 add_select_fusion.4
  58.2 6.6 %collective-permute-start.7 = (f32[10,128,64]{1,2,0:T(8,128)}, f32[10,128,64]{1,2,0:T(8,128)}, u32[]{:S(2)}, u32[]{:S(2)}) collective-permute-start(f32[10,128,64]{1,2,0:T(8,128)} %add_select_fusion.4), channel_id=1, source_target_pairs={{0,16},{8,24},{16,32},{24,40},{32,48},{40,56},{48,64},{56,72},{64,... | collective-permute-start | bytes 983048 | tf_op jit(solution)/shard_map/ppermute | solution.py:22
  64.7 5.0 %collective-permute-start.1 = (f32[10]{0:T(128)S(1)}, f32[10]{0:T(128)S(1)}, u32[]{:S(2)}, u32[]{:S(2)}) collective-permute-start(f32[10]{0:T(128)S(1)} %broadcast_select_fusion.1), channel_id=1, source_target_pairs={{0,8},{8,16},{16,24},{24,32},{32,40},{40,48},{48,56},{56,64},{64,7... | collective-permute-start | bytes 128 | tf_op jit(solution)/shard_map/ppermute | solution.py:22
  69.7 0.7 collective-permute-done.1
  70.5 1.9 add_select_fusion.3
  72.4 20.3 %collective-permute-start.8 = (f32[10,128,64]{1,2,0:T(8,128)}, f32[10,128,64]{1,2,0:T(8,128)}, u32[]{:S(2)}, u32[]{:S(2)}) collective-permute-start(f32[10,128,64]{1,2,0:T(8,128)} %add_select_fusion.3), channel_id=1, source_target_pairs={{0,32},{8,40},{16,48},{24,56},{32,64},{40,72},{48,80},{56,88},{64,... | collective-permute-start | bytes 983048 | tf_op jit(solution)/shard_map/ppermute | solution.py:22
  92.7 2.2 fusion.22
  94.9 1.5 reshape.97
  96.5 0.9 reduce_sum.18
  97.3 0.7 reduce_window_sum.43
  98.1 1.3 collective-permute-start.2
  99.4 7.2 %collective-permute-done.2 = f32[10]{0:T(128)S(1)} collective-permute-done((f32[10]{0:T(128)}, f32[10]{0:T(128)S(1)}, u32[]{:S(2)}, u32[]{:S(2)}) %collective-permute-start.2) | collective-permute-done | bytes 72 | tf_op jit(solution)/shard_map/ppermute | solution.py:22
  106.6 0.6 broadcast_select_fusion.2
  107.2 1.9 add_select_fusion.2
  109.1 5.6 %collective-permute-start.9 = (f32[10,128,64]{1,2,0:T(8,128)}, f32[10,128,64]{1,2,0:T(8,128)}, u32[]{:S(2)}, u32[]{:S(2)}) collective-permute-start(f32[10,128,64]{1,2,0:T(8,128)} %add_select_fusion.2), channel_id=1, source_target_pairs={{0,64},{8,72},{16,80},{24,88},{32,96},{40,104},{48,112},{56,120},{... | collective-permute-start | bytes 983048 | tf_op jit(solution)/shard_map/ppermute | solution.py:22
  114.7 0.7 exponential_bitcast_fusion
  115.4 0.1 copy.38
  115.5 3.8 %collective-permute-start.3 = (f32[10]{0:T(128)}, f32[10]{0:T(128)S(1)}, u32[]{:S(2)}, u32[]{:S(2)}) collective-permute-start(f32[10]{0:T(128)} %copy-done.13), channel_id=1, source_target_pairs={{0,32},{8,40},{16,48},{24,56},{32,64},{40,72},{48,80},{56,88},{64,... | collective-permute-start | bytes 128 | tf_op jit(solution)/shard_map/ppermute | solution.py:22
  119.3 0.9 collective-permute-done.3
  120.2 0.7 broadcast_select_fusion.3
  120.9 1.2 add_select_fusion.1
  122.1 8.7 %collective-permute-start.10 = (f32[10,128,64]{1,2,0:T(8,128)S(1)}, f32[10,128,64]{1,2,0:T(8,128)S(1)}, u32[]{:S(2)}, u32[]{:S(2)}) collective-permute-start(f32[10,128,64]{1,2,0:T(8,128)S(1)} %add_select_fusion.1), channel_id=1, source_target_pairs={{0,128},{8,136},{16,144},{24,152},{32,160},{40,168},{48,176},{56,1... | collective-permute-start | bytes 983048 | tf_op jit(solution)/shard_map/ppermute | solution.py:22
  130.8 0.6 iota_compare_fusion
  131.4 1.3 collective-permute-start.4
  132.7 3.3 %collective-permute-done.4 = f32[10]{0:T(128)S(1)} collective-permute-done((f32[10]{0:T(128)S(1)}, f32[10]{0:T(128)S(1)}, u32[]{:S(2)}, u32[]{:S(2)}) %collective-permute-start.4) | collective-permute-done | bytes 72 | tf_op jit(solution)/shard_map/ppermute | solution.py:22
  136.0 0.8 add_select_fusion
  136.9 2.0 copy.40
  138.9 0.0 copy-start.14
  139.0 4.4 %fusion.12 = f32[4,10,64,256]{3,2,0,1:T(8,128)S(1)} fusion(bf16[4,256,128,1]{2,1,0,3:T(8,128)(2,1)S(1)} %bitcast.48, f32[4,10,128,64]{3,2,1,0:T(8,128)} %get-tuple-element.33, f32[10,128,64]{2,1,0:T(8,128)} %copy.40, f32[4,10]{1,0:T(4,128)S(1)} %copy.38), kind=kOutput, calls=%fused_computation.18 | convolution fusion | flops 1007288320 | bytes 4522144 | tf_op jit(solution)/shard_map/cin,chnp->hpci/dot_general | solution.py:85
  143.4 4.0 %fusion.11 = bf16[10,64,4,256]{3,1,2,0:T(8,128)(2,1)S(1)} fusion(f32[4,10,64,256]{3,2,0,1:T(8,128)S(1)} %fusion.12, f32[10,4,256]{2,1,0:T(4,128)S(1)} %copy-done.9, f32[10,4,256]{2,1,0:T(4,128)S(1)} %copy-done.7, f32[4,256,256]{2,1,0:T(8,128)S(1)} %copy-done.2, pred[256,256]{1,0:T(8,128)(4,1)S(1)} %copy-done.10, bf16[10,64,4,256]{3,2,1,0:T(4,128)(2,1)S(1)} %copy-done.1, ...), kind=kOutput, calls=%fused_computation.17 | convolution fusion | flops 355205120 | bytes 6479912 | tf_op jit(solution)/shard_map/hcij,hpcj->hpci/dot_general | solution.py:61
  147.4 1.0 copy.43
  148.4 0.3 copy.47
  148.7 5.3 %stack.3 = bf16[8,640,1024]{2,1,0:T(8,128)(2,1)} broadcast(bf16[640,1024]{1,0:T(8,128)(2,1)S(1)} %bitcast.44), dimensions={1,2} | broadcast | bytes 11796480 | tf_op jit(solution)/shard_map/stack | solution.py:12
  154.0 124.7 %all_to_all.5 = bf16[8,640,1024]{2,1,0:T(8,128)(2,1)S(1)} all-to-all(bf16[8,640,1024]{2,1,0:T(8,128)(2,1)} %stack.3), channel_id=1, replica_groups=mesh['seq'=32,'grp'=8] {'grp'}, dimensions={0} | all-to-all | bytes 20971520 | tf_op jit(solution)/shard_map/all_to_all | solution.py:13
  278.8 4.5 %convolution_convert_fusion = bf16[1024,320]{0,1:T(8,128)(2,1)} fusion(bf16[5120,320]{0,1:T(8,128)(2,1)S(1)} %copy-done, bf16[5120,1024]{1,0:T(8,128)(2,1)S(1)} %bitcast.42), kind=kOutput, calls=%fused_computation.23 | convolution fusion | flops 3355770880 | bytes 14417920 | tf_op jit(solution)/shard_map/kt,kd->td/dot_general | solution.py:90
  (52 shorter events, 0.3 us)
Async XLA Ops:
  0.0 278.8 %copy-start = (bf16[5120,320]{0,1:T(8,128)(2,1)S(1)}, bf16[5120,320]{0,1:T(8,128)(2,1)}, u32[]{:S(2)}) copy-start(bf16[5120,320]{0,1:T(8,128)(2,1)} %param.15) | copy-start | bytes 9830404
  1.0 16.6 %copy-start.8 = (f32[10,4,256]{2,1,0:T(4,128)}, f32[10,4,256]{2,1,0:T(4,128)S(1)}, u32[]{:S(2)}) copy-start(f32[10,4,256]{2,1,0:T(4,128)S(1)} %mul.141) | copy-start | bytes 122884
  2.1 0.6 copy-start.5
  5.4 12.1 %copy-start.6 = (f32[10,4,256]{2,1,0:T(4,128)}, f32[10,4,256]{2,1,0:T(4,128)S(1)}, u32[]{:S(2)}) copy-start(f32[10,4,256]{2,1,0:T(4,128)S(1)} %reduce_window_sum.42) | copy-start | bytes 122884
  33.3 59.4 %copy-start.3 = (bf16[1024,128]{1,0:T(8,128)(2,1)S(1)}, bf16[1024,128]{1,0:T(8,128)(2,1)}, u32[]{:S(2)}) copy-start(bf16[1024,128]{1,0:T(8,128)(2,1)} %param.13) | copy-start | bytes 786436
  35.4 11.0 %collective-permute-start.5 = (f32[10,128,64]{1,2,0:T(8,128)}, f32[10,128,64]{1,2,0:T(8,128)}, u32[]{:S(2)}, u32[]{:S(2)}) collective-permute-start(f32[10,128,64]{1,2,0:T(8,128)} %copy.39), channel_id=1, source_target_pairs={{0,8},{8,16},{16,24},{24,32},{32,40},{40,48},{48,56},{56,64},{64,7... | collective-permute-start | bytes 983048 | tf_op jit(solution)/shard_map/ppermute | solution.py:22
  46.4 9.9 %collective-permute-start.6 = (f32[10,128,64]{1,2,0:T(8,128)}, f32[10,128,64]{1,2,0:T(8,128)}, u32[]{:S(2)}, u32[]{:S(2)}) collective-permute-start(f32[10,128,64]{1,2,0:T(8,128)} %collective-permute-done.5), channel_id=1, source_target_pairs={{0,8},{8,16},{16,24},{24,32},{32,40},{40,48},{48,56},{56,64},{64,7... | collective-permute-start | bytes 983048 | tf_op jit(solution)/shard_map/ppermute | solution.py:22
  51.2 5.0 %collective-permute-start = (f32[10]{0:T(128)S(1)}, f32[10]{0:T(128)S(1)}, u32[]{:S(2)}, u32[]{:S(2)}) collective-permute-start(f32[10]{0:T(128)S(1)} %negate_exponential_fusion), channel_id=1, source_target_pairs={{0,8},{8,16},{16,24},{24,32},{32,40},{40,48},{48,56},{56,64},{64,7... | collective-permute-start | bytes 128 | tf_op jit(solution)/shard_map/ppermute | solution.py:22
  58.2 12.3 %collective-permute-start.7 = (f32[10,128,64]{1,2,0:T(8,128)}, f32[10,128,64]{1,2,0:T(8,128)}, u32[]{:S(2)}, u32[]{:S(2)}) collective-permute-start(f32[10,128,64]{1,2,0:T(8,128)} %add_select_fusion.4), channel_id=1, source_target_pairs={{0,16},{8,24},{16,32},{24,40},{32,48},{40,56},{48,64},{56,72},{64,... | collective-permute-start | bytes 983048 | tf_op jit(solution)/shard_map/ppermute | solution.py:22
  64.7 5.7 %collective-permute-start.1 = (f32[10]{0:T(128)S(1)}, f32[10]{0:T(128)S(1)}, u32[]{:S(2)}, u32[]{:S(2)}) collective-permute-start(f32[10]{0:T(128)S(1)} %broadcast_select_fusion.1), channel_id=1, source_target_pairs={{0,8},{8,16},{16,24},{24,32},{32,40},{40,48},{48,56},{56,64},{64,7... | collective-permute-start | bytes 128 | tf_op jit(solution)/shard_map/ppermute | solution.py:22
  70.5 22.3 %copy-start.12 = (f32[10]{0:T(128)}, f32[10]{0:T(128)S(1)}, u32[]{:S(2)}) copy-start(f32[10]{0:T(128)S(1)} %broadcast_select_fusion) | copy-start | bytes 124
  72.4 34.8 %collective-permute-start.8 = (f32[10,128,64]{1,2,0:T(8,128)}, f32[10,128,64]{1,2,0:T(8,128)}, u32[]{:S(2)}, u32[]{:S(2)}) collective-permute-start(f32[10,128,64]{1,2,0:T(8,128)} %add_select_fusion.3), channel_id=1, source_target_pairs={{0,32},{8,40},{16,48},{24,56},{32,64},{40,72},{48,80},{56,88},{64,... | collective-permute-start | bytes 983048 | tf_op jit(solution)/shard_map/ppermute | solution.py:22
  94.9 44.0 %copy-start.4 = (bf16[1024,128]{1,0:T(8,128)(2,1)S(1)}, bf16[1024,128]{1,0:T(8,128)(2,1)}, u32[]{:S(2)}) copy-start(bf16[1024,128]{1,0:T(8,128)(2,1)} %param.14) | copy-start | bytes 786436
  98.1 8.5 %collective-permute-start.2 = (f32[10]{0:T(128)}, f32[10]{0:T(128)S(1)}, u32[]{:S(2)}, u32[]{:S(2)}) collective-permute-start(f32[10]{0:T(128)} %copy-done.12), channel_id=1, source_target_pairs={{0,16},{8,24},{16,32},{24,40},{32,48},{40,56},{48,64},{56,72},{64,... | collective-permute-start | bytes 128 | tf_op jit(solution)/shard_map/ppermute | solution.py:22
  107.2 1.9 copy-start.13
  109.1 11.8 %collective-permute-start.9 = (f32[10,128,64]{1,2,0:T(8,128)}, f32[10,128,64]{1,2,0:T(8,128)}, u32[]{:S(2)}, u32[]{:S(2)}) collective-permute-start(f32[10,128,64]{1,2,0:T(8,128)} %add_select_fusion.2), channel_id=1, source_target_pairs={{0,64},{8,72},{16,80},{24,88},{32,96},{40,104},{48,112},{56,120},{... | collective-permute-start | bytes 983048 | tf_op jit(solution)/shard_map/ppermute | solution.py:22
  115.5 4.7 %collective-permute-start.3 = (f32[10]{0:T(128)}, f32[10]{0:T(128)S(1)}, u32[]{:S(2)}, u32[]{:S(2)}) collective-permute-start(f32[10]{0:T(128)} %copy-done.13), channel_id=1, source_target_pairs={{0,32},{8,40},{16,48},{24,56},{32,64},{40,72},{48,80},{56,88},{64,... | collective-permute-start | bytes 128 | tf_op jit(solution)/shard_map/ppermute | solution.py:22
  122.1 13.9 %collective-permute-start.10 = (f32[10,128,64]{1,2,0:T(8,128)S(1)}, f32[10,128,64]{1,2,0:T(8,128)S(1)}, u32[]{:S(2)}, u32[]{:S(2)}) collective-permute-start(f32[10,128,64]{1,2,0:T(8,128)S(1)} %add_select_fusion.1), channel_id=1, source_target_pairs={{0,128},{8,136},{16,144},{24,152},{32,160},{40,168},{48,176},{56,1... | collective-permute-start | bytes 983048 | tf_op jit(solution)/shard_map/ppermute | solution.py:22
  131.4 4.6 %collective-permute-start.4 = (f32[10]{0:T(128)S(1)}, f32[10]{0:T(128)S(1)}, u32[]{:S(2)}, u32[]{:S(2)}) collective-permute-start(f32[10]{0:T(128)S(1)} %broadcast_select_fusion.3), channel_id=1, source_target_pairs={{0,64},{8,72},{16,80},{24,88},{32,96},{40,104},{48,112},{56,120},{... | collective-permute-start | bytes 128 | tf_op jit(solution)/shard_map/ppermute | solution.py:22
  138.9 4.4 %copy-start.1 = (bf16[10,64,4,256]{3,2,1,0:T(4,128)(2,1)S(1)}, bf16[10,64,4,256]{3,2,1,0:T(4,128)(2,1)}, u32[]{:S(2)}) copy-start(bf16[10,64,4,256]{3,2,1,0:T(4,128)(2,1)} %reshape.96) | copy-start | bytes 3932164
  138.9 4.4 %copy-start.2 = (f32[4,256,256]{2,1,0:T(8,128)S(1)}, f32[4,256,256]{2,1,0:T(8,128)}, u32[]{:S(2)}) copy-start(f32[4,256,256]{2,1,0:T(8,128)} %fusion.22) | copy-start | bytes 3145732
  138.9 4.5 %copy-start.7 = (f32[10,4,256]{2,1,0:T(4,128)S(1)}, f32[10,4,256]{2,1,0:T(4,128)}, u32[]{:S(2)}) copy-start(f32[10,4,256]{2,1,0:T(4,128)} %copy-done.6) | copy-start | bytes 122884
  138.9 4.5 %copy-start.9 = (f32[10,4,256]{2,1,0:T(4,128)S(1)}, f32[10,4,256]{2,1,0:T(4,128)}, u32[]{:S(2)}) copy-start(f32[10,4,256]{2,1,0:T(4,128)} %copy-done.8) | copy-start | bytes 122884
  138.9 4.5 %copy-start.10 = (pred[256,256]{1,0:T(8,128)(4,1)S(1)}, pred[256,256]{1,0:T(8,128)(4,1)}, u32[]{:S(2)}) copy-start(pred[256,256]{1,0:T(8,128)(4,1)} %iota_compare_fusion) | copy-start | bytes 196612
  138.9 4.5 %copy-start.11 = (f32[10,4,256]{2,1,0:T(4,128)S(1)}, f32[10,4,256]{2,1,0:T(4,128)}, u32[]{:S(2)}) copy-start(f32[10,4,256]{2,1,0:T(4,128)} %get-tuple-element.80) | copy-start | bytes 122884
  138.9 4.5 %copy-start.14 = (f32[10]{0:T(128)S(1)}, f32[10]{0:T(128)}, u32[]{:S(2)}) copy-start(f32[10]{0:T(128)} %param.12) | copy-start | bytes 124
